TPU v7x, 32 devices: a whole 2x2x4 slice. The times are simulated.
32 devices in a mesh: grp: 4 (over y, x), mem: 8 (over z, core).
Axes of the slice: x: 2, y: 2, z: 4, core: 2. Of those that a mesh axis runs over, the one named last changes fastest.
Arguments:
- background_tensor: bfloat16 [64, 256, 1024], P('grp', 'mem'), may hold values from -6 to 6
- reading_tally: int32 [64], P(('grp', 'mem')), may hold values from 128 to 1024, as said below
- measurement_slot: int32 [64, 1024], P(('grp', 'mem')), may hold values from 0 to 1023
- reading_datum: float32 [64, 1024], P(('grp', 'mem')), may hold values from -6 to 6
- error_precision: float32 [64, 1024], P(('grp', 'mem')), may hold values from 0.5 to 16
- reading_offset: float32 [64, 1024], P(('grp', 'mem')), may hold values from 0 to 1
Outputs:
- analysis: bfloat16 [64, 256, 1024], P('grp', 'mem')
Inputs may be any that keep to these rules, and one draw needn't show every extreme that they name: `reading_tally`: each column's live observations fill its first slots; at least one column has exactly 1024.
All inputs are finite; a program needn't handle non-finite values.
Results may differ from a plain program's by a relative error of at most 0.0074.
Values may be sent and summed in bfloat16 or wider, within the bound.
A program may use at most 64 MiB of HBM per device.

v0:
```python
import jax
import jax.numpy as jnp
from jax import lax
from jax.sharding import PartitionSpec as P

NSTEPS = 5


def padded(block, sides, width):
    for axis, dim in sides:
        count = lax.axis_size(axis)
        forward = [(i, i + 1) for i in range(count - 1)]
        forward.append((count - 1, 0))
        backward = [(target, source) for source, target in forward]
        low = lax.ppermute(
            lax.slice_in_dim(block, block.shape[dim] - width, None, axis=dim), axis, forward
        )
        high = lax.ppermute(lax.slice_in_dim(block, 0, width, axis=dim), axis, backward)
        block = jnp.concatenate([low, block, high], axis=dim)
    return block


def direction_weights(shift_amount):
    toward_west = jnp.exp(-((shift_amount + 0.5) ** 2))
    own_weight = jnp.exp(-((shift_amount - 0.5) ** 2))
    toward_east = jnp.exp(-((1.5 - shift_amount) ** 2))
    return (toward_west, own_weight, toward_east)


def dense_grams(obs_rows, sample_slices):
    return jnp.einsum(
        "ekm,ejm->ekj", obs_rows, obs_rows[:, :sample_slices], preferred_element_type=jnp.float32
    )


def grams(obs_rows, sample_slices):
    return dense_grams(obs_rows, sample_slices)


def per_device(
    background_tensor,
    reading_tally,
    measurement_slot,
    reading_datum,
    error_precision,
    reading_offset,
):
    background_members = lax.all_to_all(
        background_tensor, "mem", split_axis=0, concat_axis=1, tiled=True
    )
    vertical_slices, sample_slices, vertical_numbers = background_members.shape
    obs_slots = measurement_slot.shape[1]
    model_vector32 = background_members.astype(jnp.float32)
    focal_site = jnp.sum(model_vector32, axis=1) / sample_slices
    anomaly_matrix = (model_vector32 - focal_site[:, None, :]).astype(jnp.bfloat16)
    measured_vector = jax.vmap(lambda source, picks: jnp.take(source, picks, axis=1))(
        anomaly_matrix, measurement_slot
    )
    seen_mean = jax.vmap(lambda source, picks: jnp.take(source, picks, axis=0))(
        focal_site, measurement_slot
    )
    innovation = reading_datum - seen_mean
    live_mask = (jnp.arange(obs_slots, dtype=jnp.int32)[None, :] < reading_tally[:, None]).astype(
        jnp.float32
    )
    toward_west, own_weight, toward_east = direction_weights(reading_offset)

    def rows_with(weight):
        factor = jnp.sqrt(weight * error_precision) * live_mask
        scaled = (measured_vector.astype(jnp.float32) * factor[:, None, :]).astype(jnp.bfloat16)
        shifted = (innovation * factor).astype(jnp.bfloat16)
        padding = jnp.zeros((vertical_slices, 7, obs_slots), jnp.bfloat16)
        return jnp.concatenate([scaled, shifted[:, None, :], padding], axis=1)

    own_rows = rows_with(own_weight)
    side_rows = jnp.stack([rows_with(toward_west), rows_with(toward_east)], axis=1)
    side_rows = side_rows.reshape(2 * vertical_slices, sample_slices + 8, obs_slots)
    own_gram = grams(own_rows, sample_slices)
    side_gram = grams(side_rows, sample_slices)
    widened = padded(side_gram, ((("grp", "mem"), 0),), 1)
    combined = (
        own_gram + widened[0 : 2 * vertical_slices : 2] + widened[3 : 2 * vertical_slices + 2 : 2]
    )
    identity = jnp.eye(sample_slices, dtype=jnp.float32)
    system = (sample_slices - 1) * identity[None] + combined[:, :sample_slices]
    pull_vec = combined[:, sample_slices]
    norm_value = jnp.sqrt(jnp.sum(system * system, axis=(1, 2)))
    iterate = system / norm_value[:, None, None]
    inverse = jnp.broadcast_to(identity, system.shape)
    for iteration in range(NSTEPS):
        middle = 1.5 * identity[None] - 0.5 * jnp.einsum(
            "cij,cjk->cik", inverse, iterate, precision=lax.Precision.HIGHEST
        )
        iterate = jnp.einsum("cij,cjk->cik", iterate, middle, precision=lax.Precision.HIGHEST)
        inverse = jnp.einsum("cij,cjk->cik", middle, inverse, precision=lax.Precision.HIGHEST)
    inv_root = inverse / jnp.sqrt(norm_value)[:, None, None]
    inner = jnp.einsum("cij,cj->ci", inv_root, pull_vec, precision=lax.Precision.HIGHEST)
    mean_weight = jnp.einsum("cij,cj->ci", inv_root, inner, precision=lax.Precision.HIGHEST)
    weight_matrix = (jnp.sqrt(sample_slices - 1.0) * inv_root + mean_weight[:, :, None]).astype(
        jnp.bfloat16
    )
    increment = jnp.einsum(
        "mar,mao->mro", weight_matrix, anomaly_matrix, preferred_element_type=jnp.float32
    )
    analysis = (focal_site[:, None, :] + increment).astype(jnp.bfloat16)
    return lax.all_to_all(analysis, "mem", split_axis=1, concat_axis=0, tiled=True)


def solution(mesh):
    in_specs = (
        P("grp", "mem", None),
        P(("grp", "mem")),
        P(("grp", "mem"), None),
        P(("grp", "mem"), None),
        P(("grp", "mem"), None),
        P(("grp", "mem"), None),
    )
    out_specs = P("grp", "mem", None)
    return jax.shard_map(
        per_device, mesh=mesh, in_specs=in_specs, out_specs=out_specs, check_vma=False
    )
```

profile of v0, /device:TPU:0, one launch (start us, length us, event | category | flops | bytes accessed | tf_op | source)
XLA Modules:
  0.0 122.7 jit_solution(14282105869668061557)
XLA Ops:
  0.0 6.5 %all-to-all-start = ((bf16[16,32,1024]{2,1,0:T(8,128)(2,1)}), bf16[16,32,1024]{2,1,0:T(8,128)(2,1)S(1)}, u32[]{:S(2)}, u32[]{:S(2)}) async-start(bf16[16,32,1024]{2,1,0:T(8,128)(2,1)} %param.6), calls=%async_computation | async-start | bytes 2097152 | tf_op jit(solution)/shard_map/all_to_all | solution.py:48
  6.5 0.1 pad.13.clone
  6.6 26.4 %all-to-all-done = bf16[16,32,1024]{2,1,0:T(8,128)(2,1)S(1)} async-done(((bf16[16,32,1024]{2,1,0:T(8,128)(2,1)}), bf16[16,32,1024]{2,1,0:T(8,128)(2,1)S(1)}, u32[]{:S(2)}, u32[]{:S(2)}) %all-to-all-start) | async-done | bytes 1048608 | tf_op jit(solution)/shard_map/all_to_all | solution.py:48
  33.1 0.3 convert_reduce_fusion
  33.4 0.0 copy-start
  33.4 0.0 copy-start.1
  33.5 0.0 copy-start.3
  33.5 0.0 copy-start.4
  33.5 17.7 %gather_fusion.1 = f32[2048]{0:T(1024)S(1)} fusion(f32[2,1024]{1,0:T(2,128)S(1)} %broadcast_multiply_fusion, s32[2048]{0:T(1024)S(1)} %bitcast.78), kind=kCustom, calls=%fused_computation.1 | custom fusion | bytes 32768 | tf_op jit(solution)/shard_map/vmap(jit(_take))/gather | solution.py:59
  51.2 0.1 fusion.36
  51.3 0.1 fusion.37
  51.4 0.3 copy.65
  51.6 0.3 fusion.5
  51.9 0.5 copy.66
  52.4 11.1 %gather_fusion = bf16[2048,256]{1,0:T(8,128)(2,1)S(1)} fusion(bf16[2,256,1024]{1,2,0:T(8,128)(2,1)S(1)} %copy.66, s32[2048]{0:T(1024)S(1)} %bitcast.79), kind=kCustom, calls=%fused_computation | custom fusion | bytes 2113536 | tf_op jit(solution)/shard_map/vmap(jit(_take))/gather | solution.py:56
  63.5 0.5 copy.67
  64.1 0.7 fusion.19
  64.8 0.7 maximum_bitcast_fusion
  65.5 0.2 pad_maximum_fusion
  65.7 0.2 copy.72
  66.0 0.9 fusion.3
  66.9 0.1 collective-permute-start
  66.9 5.3 %collective-permute-start.1 = (f32[1,264,256]{2,1,0:T(8,128)S(1)}, f32[1,264,256]{2,1,0:T(8,128)S(1)}, u32[]{:S(2)}, u32[]{:S(2)}) collective-permute-start(f32[1,264,256]{2,1,0:T(8,128)S(1)} %get-tuple-element.14), channel_id=1, source_target_pairs={{1,0},{2,1},{3,2},{4,3},{5,4},{6,5},{7,6},{8,7},{9,8},{10,9},{11,1... | collective-permute-start | bytes 811016 | tf_op jit(solution)/shard_map/ppermute | solution.py:18
  72.4 6.8 %collective-permute-done = f32[1,264,256]{2,1,0:T(8,128)S(1)} collective-permute-done((f32[1,264,256]{2,1,0:T(8,128)S(1)}, f32[1,264,256]{2,1,0:T(8,128)S(1)}, u32[]{:S(2)}, u32[]{:S(2)}) %collective-permute-start) | collective-permute-done | bytes 270368 | tf_op jit(solution)/shard_map/ppermute | solution.py:15
  79.2 0.0 collective-permute-done.1
  79.2 0.1 pad_maximum_fusion.1
  79.3 0.7 slice_add_fusion
  80.0 0.2 multiply_reduce_fusion
  80.2 0.7 fusion.10
  81.0 0.7 fusion.45
  81.7 0.6 fusion.29
  82.3 0.7 fusion.9
  83.0 0.7 fusion.50
  83.6 0.7 fusion.49
  84.3 0.7 fusion.8
  85.0 0.7 fusion.52
  85.6 0.7 fusion.51
  86.3 0.7 fusion.7
  87.0 0.7 fusion.54
  87.7 0.7 fusion.53
  88.3 0.7 fusion.6
  89.0 0.7 convolution_divide_fusion
  89.7 0.5 fusion.39
  90.2 0.6 fusion.40
  90.8 0.6 add_convert_fusion
  91.4 1.1 copy.74
  92.4 29.0 %all_to_all.27 = bf16[2,256,1024]{2,0,1:T(2,128)(2,1)S(1)} all-to-all(bf16[2,256,1024]{2,0,1:T(2,128)(2,1)S(1)} %copy.74), channel_id=1, replica_groups=mesh['grp'=4,'mem'=8] {'mem'}, dimensions={1} | all-to-all | bytes 2097152 | tf_op jit(solution)/shard_map/all_to_all | solution.py:106
  121.4 1.3 %copy.75 = bf16[8,2,32,1024]{3,2,1,0:T(8,128)(2,1)} copy(bf16[8,2,32,1024]{3,1,2,0:T(2,128)(2,1)S(1)} %bitcast.82) | data formatting | bytes 2097152 | tf_op jit(solution)/shard_map/all_to_all | solution.py:106
  (22 shorter events, 0.3 us)
Async XLA Ops:
  0.0 6.5 %copy-start.2 = (s32[2,1024]{1,0:T(2,128)S(1)}, s32[2,1024]{1,0:T(2,128)}, u32[]{:S(2)}) copy-start(s32[2,1024]{1,0:T(2,128)} %param.8) | copy-start | bytes 24580
  0.0 33.0 %all-to-all-start = ((bf16[16,32,1024]{2,1,0:T(8,128)(2,1)}), bf16[16,32,1024]{2,1,0:T(8,128)(2,1)S(1)}, u32[]{:S(2)}, u32[]{:S(2)}) async-start(bf16[16,32,1024]{2,1,0:T(8,128)(2,1)} %param.6), calls=%async_computation | async-start | bytes 2097152 | tf_op jit(solution)/shard_map/all_to_all | solution.py:48
  33.4 17.8 %copy-start = (f32[2,1024]{1,0:T(2,128)S(1)}, f32[2,1024]{1,0:T(2,128)}, u32[]{:S(2)}) copy-start(f32[2,1024]{1,0:T(2,128)} %param.10) | copy-start | bytes 24580
  33.4 17.8 %copy-start.1 = (f32[2,1024]{1,0:T(2,128)S(1)}, f32[2,1024]{1,0:T(2,128)}, u32[]{:S(2)}) copy-start(f32[2,1024]{1,0:T(2,128)} %param.11) | copy-start | bytes 24580
  33.5 17.7 %copy-start.3 = (f32[2,1024]{1,0:T(2,128)S(1)}, f32[2,1024]{1,0:T(2,128)}, u32[]{:S(2)}) copy-start(f32[2,1024]{1,0:T(2,128)} %param.9) | copy-start | bytes 24580
  33.5 17.7 %copy-start.4 = (s32[2]{0:T(128)S(1)}, s32[2]{0:T(128)}, u32[]{:S(2)}) copy-start(s32[2]{0:T(128)} %param.7) | copy-start | bytes 28
  66.9 12.3 %collective-permute-start = (f32[1,264,256]{2,1,0:T(8,128)S(1)}, f32[1,264,256]{2,1,0:T(8,128)S(1)}, u32[]{:S(2)}, u32[]{:S(2)}) collective-permute-start(f32[1,264,256]{2,1,0:T(8,128)S(1)} %get-tuple-element.13), channel_id=1, source_target_pairs={{0,1},{1,2},{2,3},{3,4},{4,5},{5,6},{6,7},{7,8},{8,9},{9,10},{10,1... | collective-permute-start | bytes 811016 | tf_op jit(solution)/shard_map/ppermute | solution.py:15
  66.9 12.2 %collective-permute-start.1 = (f32[1,264,256]{2,1,0:T(8,128)S(1)}, f32[1,264,256]{2,1,0:T(8,128)S(1)}, u32[]{:S(2)}, u32[]{:S(2)}) collective-permute-start(f32[1,264,256]{2,1,0:T(8,128)S(1)} %get-tuple-element.14), channel_id=1, source_target_pairs={{1,0},{2,1},{3,2},{4,3},{5,4},{6,5},{7,6},{8,7},{9,8},{10,9},{11,1... | collective-permute-start | bytes 811016 | tf_op jit(solution)/shard_map/ppermute | solution.py:18
where the time goes:
time: 123 us
  waiting for transfers between devices  33.3 us (27%)
  local copies, waits for them, and re-layouts  32.9 us (27%)
  blocking collectives  29 us (24%)
  matrix products  12.5 us (10%)
  starting transfers between devices  11.9 us (10%)
  other arithmetic  2.77 us (2%)
    all_to_all x1, blocking collectives, per_device(): lax.all_to_all(analysis, 'mem', split_axis=1, concat_axis=0, tiled=True)  29 us
    all_to_all x1, waiting for transfers between devices, per_device(): lax.all_to_all(background_tensor, 'mem', split_axis=0, concat_axis=1, til...  26.4 us
    gather x2, local copies, waits for them, and re-layouts, per_device(): jnp.take(source, picks, axis=0)  17.7 us
    gather x2, local copies, waits for them, and re-layouts, per_device(): jnp.take(source, picks, axis=1)  11.6 us
    ppermute x1, waiting for transfers between devices, padded(): lax.ppermute(lax.slice_in_dim(block, block.shape[dim] - width, None, axis...  6.83 us
    all_to_all x1, starting transfers between devices, per_device(): lax.all_to_all(background_tensor, 'mem', split_axis=0, concat_axis=1, til...  6.49 us
    ppermute x1, starting transfers between devices, padded(): lax.ppermute(lax.slice_in_dim(block, 0, width, axis=dim), axis, backward)  5.33 us
    dot_general x5, matrix products, per_device(): jnp.einsum('cij,cjk->cik', inverse, iterate, precision=lax.Precision.HIGH...  3.38 us
  transfers between devices with their start and end apart: 3, of which 2 were waited for; matrix products, arithmetic and copies ran while one was open for 0% of the time, Pallas kernels for 0%

commit v1 on v0

v1 whole, which is shorter than its diff:
```python
import jax
import jax.numpy as jnp
from jax import lax
from jax.sharding import PartitionSpec as P

NSTEPS = 5
F32 = jnp.float32
BF16 = jnp.bfloat16


def slot_terms(slots, tally, datum, precision, offset):
    live = (jnp.arange(slots.shape[1], dtype=jnp.int32)[None, :] < tally[:, None]).astype(F32)
    base = precision * live
    weights = [
        jnp.exp(-((offset + 0.5) ** 2)) * base,
        jnp.exp(-((offset - 0.5) ** 2)) * base,
        jnp.exp(-((1.5 - offset) ** 2)) * base,
    ]
    return jnp.stack(weights + [w * datum for w in weights], axis=1)


def split(x):
    high = lax.reduce_precision(x, 8, 7)
    return high.astype(BF16), (x - high).astype(BF16)


def regroup(terms, slots, values):
    picks = (
        jnp.arange(values, dtype=jnp.int32)[None, :, None] == slots[:, None, :]
    ).astype(BF16)
    high, low = split(terms)
    both = jnp.concatenate([high, low], axis=1)
    sums = jnp.einsum("ctm,cvm->ctv", both, picks, preferred_element_type=F32)
    return sums[:, : terms.shape[1]] + sums[:, terms.shape[1] :]


def shifted(block, axes, up):
    sizes = [lax.axis_size(axis) for axis in axes]
    count = 1
    for size in sizes:
        count *= size
    pairs = [(i, (i + 1) % count) for i in range(count)]
    if not up:
        pairs = [(target, source) for source, target in pairs]
    return lax.ppermute(block, axes, pairs)


def plain(background, tally, slots, datum, precision, offset):
    values = background.shape[2]
    sums = regroup(slot_terms(slots, tally, datum, precision, offset), slots, values)
    members = lax.all_to_all(background, "mem", split_axis=0, concat_axis=1, tiled=True)
    columns, count, _ = members.shape
    wide = members.astype(F32)
    center = jnp.sum(wide, axis=1) / count
    spread = (wide - center[:, None, :]).astype(BF16)

    def gram(which):
        weight = sums[:, which]
        scaled = (spread.astype(F32) * weight[:, None, :]).astype(BF16)
        pulls = sums[:, which + 3] - weight * center
        high, low = split(pulls)
        padding = jnp.zeros((columns, 6, values), BF16)
        rows = jnp.concatenate([scaled, high[:, None], low[:, None], padding], axis=1)
        return jnp.einsum("ekv,ejv->ekj", rows, spread, preferred_element_type=F32)

    west, own, east = gram(0), gram(1), gram(2)
    from_east = jnp.concatenate([west[1:], shifted(west[:1], ("grp", "mem"), False)], axis=0)
    from_west = jnp.concatenate([shifted(east[-1:], ("grp", "mem"), True), east[:-1]], axis=0)
    combined = own + from_east + from_west
    identity = jnp.eye(count, dtype=F32)
    system = (count - 1) * identity[None] + combined[:, :count]
    pull = combined[:, count] + combined[:, count + 1]
    norm = jnp.sqrt(jnp.sum(system * system, axis=(1, 2)))

    def product(a, b):
        return jnp.einsum("cij,cjk->cik", a, b, precision=lax.Precision.HIGH)

    iterate = system / norm[:, None, None]
    inverse = None
    for step in range(NSTEPS):
        last = step == NSTEPS - 1
        middle = 1.5 * identity[None] - 0.5 * (
            iterate if inverse is None else product(inverse, iterate)
        )
        if not last:
            iterate = product(iterate, middle)
        inverse = middle if inverse is None else product(middle, inverse)
    root = inverse / jnp.sqrt(norm)[:, None, None]
    inner = jnp.einsum("cij,cj->ci", root, pull, precision=lax.Precision.HIGHEST)
    mean = jnp.einsum("cij,cj->ci", root, inner, precision=lax.Precision.HIGHEST)
    transform = (jnp.sqrt(count - 1.0) * root + mean[:, :, None]).astype(BF16)
    increment = jnp.einsum("cjk,cjv->ckv", transform, spread, preferred_element_type=F32)
    analysis = (center[:, None, :] + increment).astype(BF16)
    return lax.all_to_all(analysis, "mem", split_axis=1, concat_axis=0, tiled=True)


def solution(mesh):
    rows = P(("grp", "mem"), None)
    in_specs = (P("grp", "mem", None), P(("grp", "mem")), rows, rows, rows, rows)
    return jax.shard_map(
        plain, mesh=mesh, in_specs=in_specs, out_specs=P("grp", "mem", None), check_vma=False
    )
```

time: 123 us -> 87.2 us (0.71)
  local copies, waits for them, and re-layouts: 32.9 us -> 2.96 us
  waiting for transfers between devices: 33.3 us -> 29.9 us
  matrix products: 12.5 us -> 10.1 us
    gather x4 -> x0, local copies, waits for them, and re-layouts: 29.3 us -> none  [the longest x2 17.7 us: per_device(): jnp.take(source, picks, axis=0)]
    dot_general x19, matrix products: 12.5 us -> 10.1 us  [the longest x12 5.03 us: product(): return jnp.einsum('cij,cjk->cik', a, b, precision=lax.Precision.HIGH)]
    all_to_all x1, waiting for transfers between devices: 26.4 us -> 24.6 us  [plain(): lax.all_to_all(background, 'mem', split_axis=0, concat_axis=1, tiled=True)]
    ppermute x2, waiting for transfers between devices: 6.83 us -> 5.33 us  [shifted(): return lax.ppermute(block, axes, pairs)]
  transfers between devices with their start and end apart: 3 -> 3, of which waited for: 2 -> 2; matrix products, arithmetic and copies ran while one was open for 0% -> 3% of each run, Pallas kernels for 0% -> 0%
where the time goes in v1:
time: 87.2 us; the launch traced here: 87 us
  blocking collectives  30 us (34%)
  waiting for transfers between devices  29.9 us (34%)
  starting transfers between devices  12.1 us (14%)
  matrix products  10.1 us (12%)
  local copies, waits for them, and re-layouts  2.96 us (3%)
  other arithmetic  1.55 us (2%)
    all_to_all x1, blocking collectives, plain(): lax.all_to_all(analysis, 'mem', split_axis=1, concat_axis=0, tiled=True)  30 us
    all_to_all x1, waiting for transfers between devices, plain(): lax.all_to_all(background, 'mem', split_axis=0, concat_axis=1, tiled=True)  24.6 us
    all_to_all x1, starting transfers between devices, plain(): lax.all_to_all(background, 'mem', split_axis=0, concat_axis=1, tiled=True)  6.51 us
    ppermute x2, starting transfers between devices, shifted(): return lax.ppermute(block, axes, pairs)  5.62 us
    ppermute x2, waiting for transfers between devices, shifted(): return lax.ppermute(block, axes, pairs)  5.33 us
    dot_general x12, matrix products, product(): return jnp.einsum('cij,cjk->cik', a, b, precision=lax.Precision.HIGH)  5.03 us
    dot_general x3, matrix products, gram(): return jnp.einsum('ekv,ejv->ekj', rows, spread, preferred_element_type=F32)  1.84 us
  transfers between devices with their start and end apart: 3, of which 2 were waited for; matrix products, arithmetic and copies ran while one was open for 3% of the time, Pallas kernels for 0%

profile of v1, /device:TPU:0, one launch (start us, length us, event | category | flops | bytes accessed | tf_op | source)
XLA Modules:
  0.0 87.0 jit_solution(4481563126192155838)
XLA Ops:
  0.0 0.0 copy-start.2
  0.0 0.0 copy-start.1
  0.0 0.0 copy-start.3
  0.0 0.0 copy-start
  0.0 0.0 copy-start.4
  0.0 6.5 %all-to-all-start = ((bf16[16,32,1024]{2,1,0:T(8,128)(2,1)}), bf16[16,32,1024]{2,1,0:T(8,128)(2,1)S(1)}, u32[]{:S(2)}, u32[]{:S(2)}) async-start(bf16[16,32,1024]{2,1,0:T(8,128)(2,1)} %param.6), calls=%async_computation | async-start | bytes 2097152 | tf_op jit(solution)/shard_map/all_to_all | solution.py:51
  6.5 0.0 copy-done.2
  6.5 0.0 copy-done.1
  6.5 0.0 copy-done.3
  6.6 0.0 copy-done
  6.6 0.1 fusion.73
  6.8 0.1 pad.15.clone
  6.8 0.1 stack.27
  6.9 0.0 copy-done.4
  7.0 1.5 %fusion = f32[2,12,1024]{2,1,0:T(8,128)S(1)} fusion(s32[2,1024]{1,0:T(2,128)S(1)} %copy-done.4, bf16[2,6,1024]{2,1,0:T(8,128)(2,1)S(1)} %get-tuple-element.27, bf16[2,6,1024]{2,1,0:T(8,128)(2,1)S(1)} %get-tuple-element.26), kind=kOutput, calls=%fused_computation.1 | convolution fusion | flops 52527104 | bytes 155648 | tf_op jit(solution)/shard_map/ctm,cvm->ctv/dot_general | solution.py:33
  8.5 24.6 %all-to-all-done = bf16[16,32,1024]{2,1,0:T(8,128)(2,1)S(1)} async-done(((bf16[16,32,1024]{2,1,0:T(8,128)(2,1)}), bf16[16,32,1024]{2,1,0:T(8,128)(2,1)S(1)}, u32[]{:S(2)}, u32[]{:S(2)}) %all-to-all-start) | async-done | bytes 1048608 | tf_op jit(solution)/shard_map/all_to_all | solution.py:51
  33.1 0.3 convert_reduce_fusion
  33.5 0.1 reduce-precision_convert_fusion.3
  33.5 0.2 copy.34
  33.8 0.4 fusion.2
  34.2 0.4 fusion.4
  34.6 0.6 fusion.24
  35.3 0.1 collective-permute-start.1
  35.4 0.6 fusion.17
  36.0 5.6 %collective-permute-start = (f32[1,264,256]{2,1,0:T(8,128)S(1)}, f32[1,264,256]{2,1,0:T(8,128)S(1)}, u32[]{:S(2)}, u32[]{:S(2)}) collective-permute-start(f32[1,264,256]{2,1,0:T(8,128)S(1)} %get-tuple-element.18), channel_id=1, source_target_pairs={{1,0},{2,1},{3,2},{4,3},{5,4},{6,5},{7,6},{8,7},{9,8},{10,9},{11,1... | collective-permute-start | bytes 811016 | tf_op jit(solution)/shard_map/ppermute | solution.py:45
  41.6 5.3 %collective-permute-done.1 = f32[1,264,256]{2,1,0:T(8,128)S(1)} collective-permute-done((f32[1,264,256]{2,1,0:T(8,128)S(1)}, f32[1,264,256]{2,1,0:T(8,128)S(1)}, u32[]{:S(2)}, u32[]{:S(2)}) %collective-permute-start.1) | collective-permute-done | bytes 270368 | tf_op jit(solution)/shard_map/ppermute | solution.py:45
  47.0 0.0 collective-permute-done
  47.0 0.6 fusion.34
  47.6 0.2 multiply_reduce_fusion
  47.8 0.5 fusion.36
  48.4 0.5 fusion.9
  48.9 0.4 fusion.81
  49.3 0.5 fusion.35
  49.8 0.4 fusion.8
  50.2 0.4 fusion.83
  50.6 0.4 fusion.82
  51.0 0.4 fusion.7
  51.4 0.4 fusion.85
  51.8 0.4 fusion.84
  52.2 0.4 fusion.6
  52.6 0.4 convolution_divide_fusion
  53.0 0.5 fusion.56
  53.5 0.6 fusion.59
  54.1 0.6 add_convert_fusion
  54.6 1.1 %copy.41 = bf16[2,256,1024]{2,0,1:T(2,128)(2,1)S(1)} copy(bf16[2,256,1024]{2,1,0:T(8,128)(2,1)S(1)} %add_convert_fusion) | data formatting | bytes 2097152 | tf_op jit(solution)/shard_map/convert_element_type | solution.py:93
  55.7 30.0 %all_to_all.27 = bf16[2,256,1024]{2,0,1:T(2,128)(2,1)S(1)} all-to-all(bf16[2,256,1024]{2,0,1:T(2,128)(2,1)S(1)} %copy.41), channel_id=1, replica_groups=mesh['grp'=4,'mem'=8] {'mem'}, dimensions={1} | all-to-all | bytes 2097152 | tf_op jit(solution)/shard_map/all_to_all | solution.py:94
  85.7 1.3 %copy.42 = bf16[8,2,32,1024]{3,2,1,0:T(8,128)(2,1)} copy(bf16[8,2,32,1024]{3,1,2,0:T(2,128)(2,1)S(1)} %bitcast.67) | data formatting | bytes 2097152 | tf_op jit(solution)/shard_map/all_to_all | solution.py:94
  (22 shorter events, 0.3 us)
Async XLA Ops:
  0.0 6.5 %copy-start.2 = (f32[2,1024]{1,0:T(2,128)S(1)}, f32[2,1024]{1,0:T(2,128)}, u32[]{:S(2)}) copy-start(f32[2,1024]{1,0:T(2,128)} %param.10) | copy-start | bytes 24580
  0.0 6.5 %copy-start.1 = (f32[2,1024]{1,0:T(2,128)S(1)}, f32[2,1024]{1,0:T(2,128)}, u32[]{:S(2)}) copy-start(f32[2,1024]{1,0:T(2,128)} %param.11) | copy-start | bytes 24580
  0.0 6.5 %copy-start.3 = (s32[2]{0:T(128)S(1)}, s32[2]{0:T(128)}, u32[]{:S(2)}) copy-start(s32[2]{0:T(128)} %param.7) | copy-start | bytes 28
  0.0 6.5 %copy-start = (f32[2,1024]{1,0:T(2,128)S(1)}, f32[2,1024]{1,0:T(2,128)}, u32[]{:S(2)}) copy-start(f32[2,1024]{1,0:T(2,128)} %param.9) | copy-start | bytes 24580
  0.0 6.9 %copy-start.4 = (s32[2,1024]{1,0:T(2,128)S(1)}, s32[2,1024]{1,0:T(2,128)}, u32[]{:S(2)}) copy-start(s32[2,1024]{1,0:T(2,128)} %param.8) | copy-start | bytes 24580
  0.0 33.1 %all-to-all-start = ((bf16[16,32,1024]{2,1,0:T(8,128)(2,1)}), bf16[16,32,1024]{2,1,0:T(8,128)(2,1)S(1)}, u32[]{:S(2)}, u32[]{:S(2)}) async-start(bf16[16,32,1024]{2,1,0:T(8,128)(2,1)} %param.6), calls=%async_computation | async-start | bytes 2097152 | tf_op jit(solution)/shard_map/all_to_all | solution.py:51
  35.3 11.7 %collective-permute-start.1 = (f32[1,264,256]{2,1,0:T(8,128)S(1)}, f32[1,264,256]{2,1,0:T(8,128)S(1)}, u32[]{:S(2)}, u32[]{:S(2)}) collective-permute-start(f32[1,264,256]{2,1,0:T(8,128)S(1)} %get-tuple-element.15), channel_id=1, source_target_pairs={{0,1},{1,2},{2,3},{3,4},{4,5},{5,6},{6,7},{7,8},{8,9},{9,10},{10,1... | collective-permute-start | bytes 811016 | tf_op jit(solution)/shard_map/ppermute | solution.py:45
  36.0 11.0 %collective-permute-start = (f32[1,264,256]{2,1,0:T(8,128)S(1)}, f32[1,264,256]{2,1,0:T(8,128)S(1)}, u32[]{:S(2)}, u32[]{:S(2)}) collective-permute-start(f32[1,264,256]{2,1,0:T(8,128)S(1)} %get-tuple-element.18), channel_id=1, source_target_pairs={{1,0},{2,1},{3,2},{4,3},{5,4},{6,5},{7,6},{8,7},{9,8},{10,9},{11,1... | collective-permute-start | bytes 811016 | tf_op jit(solution)/shard_map/ppermute | solution.py:45

commit v2 on v1

--- a/solution.py
+++ b/solution.py
@@ -1,6 +1,10 @@
+import functools
+
 import jax
 import jax.numpy as jnp
 from jax import lax
+from jax.experimental import pallas as pl
+from jax.experimental.pallas import tpu as pltpu
 from jax.sharding import PartitionSpec as P
 
 NSTEPS = 5
@@ -94,9 +98,304 @@
     return lax.all_to_all(analysis, "mem", split_axis=1, concat_axis=0, tiled=True)
 
 
+NT = (((1,), (1,)), ((), ()))
+NN = (((1,), (0,)), ((), ()))
+PAD = 16
+TILE = 256
+
+
+def dot(a, b, dims=NN):
+    return lax.dot_general(a, b, dims, preferred_element_type=F32)
+
+
+def halves(x):
+    high = x.astype(BF16)
+    return high, (x - high.astype(F32)).astype(BF16)
+
+
+def product(a, b):
+    (ah, al), (bh, bl) = a, b
+    return dot(ah, bh) + (dot(ah, bl) + dot(al, bh))
+
+
+def fused_kernel(
+    groups,
+    ranks,
+    tally_ref,
+    slot_ref,
+    datum_ref,
+    precision_ref,
+    offset_ref,
+    back_ref,
+    out_ref,
+    got,
+    spread,
+    center,
+    sums,
+    rows,
+    gram,
+    from_east,
+    from_west,
+    stage,
+    bufs,
+    in_send,
+    in_recv,
+    out_send,
+    out_recv,
+    own_sem,
+    side_send,
+    side_recv,
+):
+    per, values = back_ref.shape[1], back_ref.shape[2]
+    count = ranks * per
+    height = count + PAD
+    g, r = lax.axis_index("grp"), lax.axis_index("mem")
+    total = groups * ranks
+    place = g * ranks + r
+    ahead = lax.rem(place + 1, total)
+    behind = lax.rem(place + total - 1, total)
+    east_id = (ahead // ranks, lax.rem(ahead, ranks))
+    west_id = (behind // ranks, lax.rem(behind, ranks))
+
+    barrier = pltpu.get_barrier_semaphore()
+
+    def greet(where):
+        pl.semaphore_signal(
+            barrier, inc=1, device_id=where, device_id_type=pl.DeviceIdType.MESH
+        )
+
+    for i in range(1, ranks):
+        greet((g, lax.rem(r + i, ranks)))
+    greet(east_id)
+    greet(west_id)
+    pl.semaphore_wait(barrier, ranks + 1)
+
+    def inward(c, i):
+        to = lax.rem(r + i, ranks)
+        return pltpu.make_async_remote_copy(
+            src_ref=back_ref.at[2 * to + c],
+            dst_ref=got.at[c, r],
+            send_sem=in_send.at[c, i],
+            recv_sem=in_recv.at[c, i],
+            device_id=(g, to),
+            device_id_type=pl.DeviceIdType.MESH,
+        )
+
+    def outward(c, i):
+        to = lax.rem(r + i, ranks)
+        return pltpu.make_async_remote_copy(
+            src_ref=stage.at[c, to],
+            dst_ref=out_ref.at[2 * r + c],
+            send_sem=out_send.at[c, i],
+            recv_sem=out_recv.at[c, i],
+            device_id=(g, to),
+            device_id_type=pl.DeviceIdType.MESH,
+        )
+
+    def own_in(c):
+        return pltpu.make_async_copy(back_ref.at[2 * r + c], got.at[c, r], own_sem.at[c])
+
+    def own_out(c):
+        return pltpu.make_async_copy(stage.at[c, r], out_ref.at[2 * r + c], own_sem.at[2 + c])
+
+    def sideways(k, start_row, c, landing, where):
+        return pltpu.make_async_remote_copy(
+            src_ref=gram.at[c, pl.ds(start_row, height)],
+            dst_ref=landing,
+            send_sem=side_send.at[k],
+            recv_sem=side_recv.at[k],
+            device_id=where,
+            device_id_type=pl.DeviceIdType.MESH,
+        )
+
+    for c in range(2):
+        for i in range(1, ranks):
+            inward(c, i).start()
+        own_in(c).start()
+
+    lane = lax.broadcasted_iota(jnp.int32, (1, slot_ref.shape[1]), 1)
+    row8 = lax.broadcasted_iota(jnp.int32, (8, slot_ref.shape[1]), 0)
+    for c in range(2):
+        base = jnp.where(lane < tally_ref[c], precision_ref[c : c + 1, :], 0.0)
+        offset = offset_ref[c : c + 1, :]
+        datum = datum_ref[c : c + 1, :]
+        terms = [
+            jnp.exp(-((offset + 0.5) ** 2)) * base,
+            jnp.exp(-((offset - 0.5) ** 2)) * base,
+            jnp.exp(-((1.5 - offset) ** 2)) * base,
+        ]
+        terms = terms + [t * datum for t in terms]
+        stacked = jnp.zeros(row8.shape, F32)
+        for k, term in enumerate(terms):
+            stacked = jnp.where(row8 == k, term, stacked)
+        high, low = halves(stacked)
+        slots = slot_ref[c : c + 1, :]
+
+        def collect(t, carry):
+            start = pl.multiple_of(t * TILE, TILE)
+            value = lax.broadcasted_iota(jnp.int32, (TILE, slots.shape[1]), 0) + start
+            picks = jnp.where(value == slots, 1.0, 0.0).astype(BF16)
+            sums[c, :, pl.ds(start, TILE)] = dot(high, picks, NT) + dot(low, picks, NT)
+            return carry
+
+        lax.fori_loop(0, values // TILE, collect, 0)
+
+    row16 = lax.broadcasted_iota(jnp.int32, (PAD, TILE), 0)
+
+    def grams(c):
+        own_in(c).wait()
+        for i in range(1, ranks):
+            inward(c, i).wait_recv()
+
+        def prepare(t, carry):
+            start = pl.multiple_of(t * TILE, TILE)
+            here = pl.ds(start, TILE)
+            wide = got[c, :, :, here].reshape(count, TILE).astype(F32)
+            middle = jnp.sum(wide, axis=0, keepdims=True) / count
+            center[c, :, here] = middle
+            away = (wide - middle).astype(BF16)
+            spread[c, :, here] = away
+            away = away.astype(F32)
+            for k in range(3):
+                weight = sums[c, k : k + 1, here]
+                high, low = halves(sums[c, k + 3 : k + 4, here] - weight * middle)
+                rows[k * height : k * height + count, here] = (away * weight).astype(BF16)
+                pulls = jnp.where(
+                    row16 == 0, high.astype(F32), jnp.where(row16 == 1, low.astype(F32), 0.0)
+                )
+                rows[k * height + count : (k + 1) * height, here] = pulls.astype(BF16)
+            return carry
+
+        lax.fori_loop(0, values // TILE, prepare, 0)
+        for k in range(3):
+            gram[c, k * height : (k + 1) * height, :] = dot(
+                rows[k * height : (k + 1) * height, :], spread[c], NT
+            )
+
+    grams(0)
+    westward = sideways(0, 0, 0, from_east, west_id)
+    westward.start()
+    grams(1)
+    eastward = sideways(1, 2 * height, 1, from_west, east_id)
+    eastward.start()
+
+    square = (
+        lax.broadcasted_iota(jnp.int32, (count, count), 0)
+        == lax.broadcasted_iota(jnp.int32, (count, count), 1)
+    )
+
+    def middle_of(x):
+        return jnp.where(square, 1.5, 0.0) - 0.5 * x
+
+    def analyse(c, west_part, east_part):
+        def combined(start, size):
+            at = pl.ds(start, size)
+            return gram[c, pl.ds(height + start, size), :] + west_part(at) + east_part(at)
+
+        system = combined(0, count) + jnp.where(square, count - 1.0, 0.0)
+        pulls = combined(count, 8)
+        pull = pulls[0:1] + pulls[1:2]
+        norm = jnp.sqrt(
+            jnp.sum(jnp.sum(system * system, axis=1, keepdims=True), axis=0, keepdims=True)
+        )
+        first = system * (1.0 / norm)
+        factor = middle_of(first)
+        pair = halves(factor)
+        bufs[0] = product(halves(first), pair)
+        bufs[1] = factor
+
+        def step(t, carry):
+            iterate, inverse = halves(bufs[0]), halves(bufs[1])
+            pair = halves(middle_of(product(inverse, iterate)))
+            bufs[0] = product(iterate, pair)
+            bufs[1] = product(pair, inverse)
+            return carry
+
+        lax.fori_loop(0, NSTEPS - 2, step, 0)
+        iterate, inverse = halves(bufs[0]), halves(bufs[1])
+        pair = halves(middle_of(product(inverse, iterate)))
+        root = product(pair, inverse) * (1.0 / jnp.sqrt(norm))
+        pair = halves(root)
+        inner = product(halves(jnp.broadcast_to(pull, (8, count))), pair)
+        mean = product(halves(inner), pair)[0:1]
+        transform = (root * (count - 1.0) ** 0.5 + mean).astype(BF16)
+
+        def apply(t, carry):
+            here = pl.ds(pl.multiple_of(t * TILE, TILE), TILE)
+            result = center[c, :, here] + dot(transform, spread[c, :, here])
+            stage[c, :, :, here] = result.astype(BF16).reshape(ranks, per, TILE)
+            return carry
+
+        lax.fori_loop(0, values // TILE, apply, 0)
+        for i in range(1, ranks):
+            outward(c, i).start()
+        own_out(c).start()
+
+    westward.wait_recv()
+    analyse(1, lambda at: gram[0, pl.ds(2 * height + at.start, at.size), :], lambda at: from_east[at, :])
+    eastward.wait_recv()
+    analyse(0, lambda at: from_west[at, :], lambda at: gram[1, at, :])
+    westward.wait_send()
+    eastward.wait_send()
+    for c in range(2):
+        own_out(c).wait()
+        for i in range(1, ranks):
+            inward(c, i).wait_send()
+    for c in range(2):
+        for i in range(1, ranks):
+            outward(c, i).wait()
+
+
+def fused(groups, ranks, background, tally, slots, datum, precision, offset):
+    _, per, values = background.shape
+    count = ranks * per
+    height = count + PAD
+    vmem = pl.BlockSpec(memory_space=pltpu.VMEM)
+    hbm = pl.BlockSpec(memory_space=pl.ANY)
+    smem = pl.BlockSpec(memory_space=pltpu.SMEM)
+    dma = pltpu.SemaphoreType.DMA
+    return pl.pallas_call(
+        functools.partial(fused_kernel, groups, ranks),
+        out_shape=jax.ShapeDtypeStruct(background.shape, background.dtype),
+        in_specs=[smem, vmem, vmem, vmem, vmem, hbm],
+        out_specs=hbm,
+        scratch_shapes=[
+            pltpu.VMEM((2, ranks, per, values), BF16),
+            pltpu.VMEM((2, count, values), BF16),
+            pltpu.VMEM((2, 1, values), F32),
+            pltpu.VMEM((2, 8, values), F32),
+            pltpu.VMEM((3 * height, values), BF16),
+            pltpu.VMEM((2, 3 * height, count), F32),
+            pltpu.VMEM((height, count), F32),
+            pltpu.VMEM((height, count), F32),
+            pltpu.VMEM((2, ranks, per, values), BF16),
+            pltpu.VMEM((2, count, count), F32),
+            dma((2, ranks)),
+            dma((2, ranks)),
+            dma((2, ranks)),
+            dma((2, ranks)),
+            dma((4,)),
+            dma((2,)),
+            dma((2,)),
+        ],
+        compiler_params=pltpu.CompilerParams(
+            collective_id=0, has_side_effects=True, vmem_limit_bytes=48 * 1024 * 1024
+        ),
+    )(tally, slots, datum, precision, offset, background)
+
+
+def per_device(groups, ranks, background, tally, slots, datum, precision, offset):
+    columns, per, values = background.shape
+    whole_tiles = per % 16 == 0 and values % TILE == 0 and (ranks * per) % 128 == 0
+    if columns == 2 * ranks and whole_tiles and groups * ranks > 2:
+        return fused(groups, ranks, background, tally, slots, datum, precision, offset)
+    return plain(background, tally, slots, datum, precision, offset)
+
+
 def solution(mesh):
     rows = P(("grp", "mem"), None)
     in_specs = (P("grp", "mem", None), P(("grp", "mem")), rows, rows, rows, rows)
+    body = functools.partial(per_device, mesh.shape["grp"], mesh.shape["mem"])
     return jax.shard_map(
-        plain, mesh=mesh, in_specs=in_specs, out_specs=P("grp", "mem", None), check_vma=False
+        body, mesh=mesh, in_specs=in_specs, out_specs=P("grp", "mem", None), check_vma=False
     )

time: 87.2 us -> 67.2 us (0.77)
  the two profiles are of different devices: /device:TPU:0 before, /device:TPU:15 now
where the time goes in v2:
time: 67.2 us; the launch traced here: 66.8 us
  Pallas kernels  61.2 us (91%)
  local copies, waits for them, and re-layouts  5.64 us (8%)
    pallas_call x1, Pallas kernels, fused(): pl.pallas_call(functools.partial(fused_kernel, groups, ranks), out_shape=...  61.2 us
    unnamed x13, local copies, waits for them, and re-layouts  5.64 us

profile of v2, /device:TPU:15, one launch (start us, length us, event | category | flops | bytes accessed | tf_op | source)
XLA Modules:
  0.0 66.8 jit_solution(17623352254454409537)
XLA Ops:
  0.0 0.0 copy-start
  0.0 1.2 %copy-done = bf16[16,32,1024]{2,1,0:T(8,128)(2,1)S(1)} copy-done((bf16[16,32,1024]{2,1,0:T(8,128)(2,1)S(1)}, bf16[16,32,1024]{2,1,0:T(8,128)(2,1)}, u32[]{:S(2)}) %copy-start) | copy-done | bytes 1048600
  1.2 0.0 copy-start.1
  1.2 0.7 %copy-done.1 = s32[2,1024]{1,0:T(2,128)S(1)} copy-done((s32[2,1024]{1,0:T(2,128)S(1)}, s32[2,1024]{1,0:T(2,128)}, u32[]{:S(2)}) %copy-start.1) | copy-done | bytes 8216
  1.9 0.0 copy-start.2
  1.9 0.7 %copy-done.2 = f32[2,1024]{1,0:T(2,128)S(1)} copy-done((f32[2,1024]{1,0:T(2,128)S(1)}, f32[2,1024]{1,0:T(2,128)}, u32[]{:S(2)}) %copy-start.2) | copy-done | bytes 8216
  2.6 0.0 copy-start.3
  2.6 0.7 %copy-done.3 = f32[2,1024]{1,0:T(2,128)S(1)} copy-done((f32[2,1024]{1,0:T(2,128)S(1)}, f32[2,1024]{1,0:T(2,128)}, u32[]{:S(2)}) %copy-start.3) | copy-done | bytes 8216
  3.3 0.0 copy-start.4
  3.3 0.7 %copy-done.4 = f32[2,1024]{1,0:T(2,128)S(1)} copy-done((f32[2,1024]{1,0:T(2,128)S(1)}, f32[2,1024]{1,0:T(2,128)}, u32[]{:S(2)}) %copy-start.4) | copy-done | bytes 8216
  4.0 0.0 copy-start.5
  4.0 0.7 copy-done.5
  4.7 61.2 %shard_map.64 = bf16[16,32,1024]{2,1,0:T(8,128)(2,1)S(1)} custom-call(s32[2]{0:T(128)S(1)} %copy-done.5, s32[2,1024]{1,0:T(2,128)S(1)} %copy-done.1, f32[2,1024]{1,0:T(2,128)S(1)} %copy-done.2, f32[2,1024]{1,0:T(2,128)S(1)} %copy-done.3, f32[2,1024]{1,0:T(2,128)S(1)} %copy-done.4, bf16[16,32,1024]{2,1,0:T(8,128)(2,1)S(1)} %copy-done), custom_call_target="tpu_custom_call" | custom-call | tf_op jit(solution)/shard_map/pallas_call | solution.py:357
  65.9 1.0 %copy.8 = bf16[16,32,1024]{2,1,0:T(8,128)(2,1)} copy(bf16[16,32,1024]{2,1,0:T(8,128)(2,1)S(1)} %shard_map.64) | data formatting | bytes 2097152
Async XLA Ops:
  0.0 1.2 %copy-start = (bf16[16,32,1024]{2,1,0:T(8,128)(2,1)S(1)}, bf16[16,32,1024]{2,1,0:T(8,128)(2,1)}, u32[]{:S(2)}) copy-start(bf16[16,32,1024]{2,1,0:T(8,128)(2,1)} %back_ref.1) | copy-start | bytes 3145732
  1.2 0.7 %copy-start.1 = (s32[2,1024]{1,0:T(2,128)S(1)}, s32[2,1024]{1,0:T(2,128)}, u32[]{:S(2)}) copy-start(s32[2,1024]{1,0:T(2,128)} %slot_ref.1) | copy-start | bytes 24580
  1.9 0.7 %copy-start.2 = (f32[2,1024]{1,0:T(2,128)S(1)}, f32[2,1024]{1,0:T(2,128)}, u32[]{:S(2)}) copy-start(f32[2,1024]{1,0:T(2,128)} %datum_ref.1) | copy-start | bytes 24580
  2.6 0.7 %copy-start.3 = (f32[2,1024]{1,0:T(2,128)S(1)}, f32[2,1024]{1,0:T(2,128)}, u32[]{:S(2)}) copy-start(f32[2,1024]{1,0:T(2,128)} %precision_ref.1) | copy-start | bytes 24580
  3.3 0.7 %copy-start.4 = (f32[2,1024]{1,0:T(2,128)S(1)}, f32[2,1024]{1,0:T(2,128)}, u32[]{:S(2)}) copy-start(f32[2,1024]{1,0:T(2,128)} %offset_ref.1) | copy-start | bytes 24580
  4.0 0.7 copy-start.5

commit v3 on v2

--- a/solution.py
+++ b/solution.py
@@ -121,19 +121,25 @@
 def fused_kernel(
     groups,
     ranks,
+    tally_hbm,
+    slot_hbm,
+    datum_hbm,
+    precision_hbm,
+    offset_hbm,
+    back_ref,
+    out_ref,
     tally_ref,
     slot_ref,
     datum_ref,
     precision_ref,
     offset_ref,
-    back_ref,
-    out_ref,
     got,
     spread,
     center,
     sums,
     rows,
     gram,
+    leaving,
     from_east,
     from_west,
     stage,
@@ -145,6 +151,7 @@
     own_sem,
     side_send,
     side_recv,
+    load_sem,
 ):
     per, values = back_ref.shape[1], back_ref.shape[2]
     count = ranks * per
@@ -157,6 +164,21 @@
     east_id = (ahead // ranks, lax.rem(ahead, ranks))
     west_id = (behind // ranks, lax.rem(behind, ranks))
 
+    loads = [
+        pltpu.make_async_copy(source, target, load_sem.at[k])
+        for k, (source, target) in enumerate(
+            [
+                (tally_hbm, tally_ref),
+                (slot_hbm, slot_ref),
+                (datum_hbm, datum_ref),
+                (precision_hbm, precision_ref),
+                (offset_hbm, offset_ref),
+            ]
+        )
+    ]
+    for load in loads:
+        load.start()
+
     barrier = pltpu.get_barrier_semaphore()
 
     def greet(where):
@@ -198,9 +220,9 @@
     def own_out(c):
         return pltpu.make_async_copy(stage.at[c, r], out_ref.at[2 * r + c], own_sem.at[2 + c])
 
-    def sideways(k, start_row, c, landing, where):
+    def sideways(k, landing, where):
         return pltpu.make_async_remote_copy(
-            src_ref=gram.at[c, pl.ds(start_row, height)],
+            src_ref=leaving.at[k],
             dst_ref=landing,
             send_sem=side_send.at[k],
             recv_sem=side_recv.at[k],
@@ -208,10 +230,16 @@
             device_id_type=pl.DeviceIdType.MESH,
         )
 
-    for c in range(2):
-        for i in range(1, ranks):
-            inward(c, i).start()
-        own_in(c).start()
+    order = list(range(1, ranks))
+    early = (len(order) + 1) // 2
+    for i in order:
+        inward(0, i).start()
+    own_in(0).start()
+    for i in order[:early]:
+        inward(1, i).start()
+    own_in(1).start()
+    for load in loads:
+        load.wait()
 
     lane = lax.broadcasted_iota(jnp.int32, (1, slot_ref.shape[1]), 1)
     row8 = lax.broadcasted_iota(jnp.int32, (8, slot_ref.shape[1]), 0)
@@ -273,10 +301,14 @@
             )
 
     grams(0)
-    westward = sideways(0, 0, 0, from_east, west_id)
+    leaving[0] = gram[0, 0:height, :].astype(BF16)
+    westward = sideways(0, from_east, west_id)
     westward.start()
+    for i in order[early:]:
+        inward(1, i).start()
     grams(1)
-    eastward = sideways(1, 2 * height, 1, from_west, east_id)
+    leaving[1] = gram[1, 2 * height : 3 * height, :].astype(BF16)
+    eastward = sideways(1, from_west, east_id)
     eastward.start()
 
     square = (
@@ -293,7 +325,7 @@
             return gram[c, pl.ds(height + start, size), :] + west_part(at) + east_part(at)
 
         system = combined(0, count) + jnp.where(square, count - 1.0, 0.0)
-        pulls = combined(count, 8)
+        pulls = combined(count, PAD)
         pull = pulls[0:1] + pulls[1:2]
         norm = jnp.sqrt(
             jnp.sum(jnp.sum(system * system, axis=1, keepdims=True), axis=0, keepdims=True)
@@ -332,9 +364,9 @@
         own_out(c).start()
 
     westward.wait_recv()
-    analyse(1, lambda at: gram[0, pl.ds(2 * height + at.start, at.size), :], lambda at: from_east[at, :])
+    analyse(1, lambda at: gram[0, pl.ds(2 * height + at.start, at.size), :], lambda at: from_east[at, :].astype(F32))
     eastward.wait_recv()
-    analyse(0, lambda at: from_west[at, :], lambda at: gram[1, at, :])
+    analyse(0, lambda at: from_west[at, :].astype(F32), lambda at: gram[1, at, :])
     westward.wait_send()
     eastward.wait_send()
     for c in range(2):
@@ -350,24 +382,29 @@
     _, per, values = background.shape
     count = ranks * per
     height = count + PAD
-    vmem = pl.BlockSpec(memory_space=pltpu.VMEM)
     hbm = pl.BlockSpec(memory_space=pl.ANY)
-    smem = pl.BlockSpec(memory_space=pltpu.SMEM)
+    observed = pltpu.VMEM(slots.shape, F32)
     dma = pltpu.SemaphoreType.DMA
     return pl.pallas_call(
         functools.partial(fused_kernel, groups, ranks),
         out_shape=jax.ShapeDtypeStruct(background.shape, background.dtype),
-        in_specs=[smem, vmem, vmem, vmem, vmem, hbm],
+        in_specs=[hbm] * 6,
         out_specs=hbm,
         scratch_shapes=[
+            pltpu.SMEM(tally.shape, jnp.int32),
+            pltpu.VMEM(slots.shape, jnp.int32),
+            observed,
+            observed,
+            observed,
             pltpu.VMEM((2, ranks, per, values), BF16),
             pltpu.VMEM((2, count, values), BF16),
             pltpu.VMEM((2, 1, values), F32),
             pltpu.VMEM((2, 8, values), F32),
             pltpu.VMEM((3 * height, values), BF16),
             pltpu.VMEM((2, 3 * height, count), F32),
-            pltpu.VMEM((height, count), F32),
-            pltpu.VMEM((height, count), F32),
+            pltpu.VMEM((2, height, count), BF16),
+            pltpu.VMEM((height, count), BF16),
+            pltpu.VMEM((height, count), BF16),
             pltpu.VMEM((2, ranks, per, values), BF16),
             pltpu.VMEM((2, count, count), F32),
             dma((2, ranks)),
@@ -377,9 +414,10 @@
             dma((4,)),
             dma((2,)),
             dma((2,)),
+            dma((5,)),
         ],
         compiler_params=pltpu.CompilerParams(
-            collective_id=0, has_side_effects=True, vmem_limit_bytes=48 * 1024 * 1024
+            collective_id=0, has_side_effects=True, vmem_limit_bytes=67043328
         ),
     )(tally, slots, datum, precision, offset, background)
 

time: 67.2 us -> 60.5 us (0.900)
  the two profiles are of different devices: /device:TPU:15 before, /device:TPU:25 now
where the time goes in v3:
time: 60.5 us; the launch traced here: 60.4 us
  Pallas kernels  58.1 us (96%)
  local copies, waits for them, and re-layouts  2.29 us (4%)
    pallas_call x1, Pallas kernels, fused(): pl.pallas_call(functools.partial(fused_kernel, groups, ranks), out_shape=...  58.1 us
    unnamed x1, local copies, waits for them, and re-layouts  2.29 us

profile of v3, /device:TPU:25, one launch (start us, length us, event | category | flops | bytes accessed | tf_op | source)
XLA Modules:
  0.0 60.4 jit_solution(12655164916992963622)
XLA Ops:
  0.0 58.1 %shard_map.64 = bf16[16,32,1024]{2,1,0:T(8,128)(2,1)} custom-call(s32[2]{0:T(128)} %tally_hbm.1, s32[2,1024]{1,0:T(2,128)} %slot_hbm.1, f32[2,1024]{1,0:T(2,128)} %datum_hbm.1, f32[2,1024]{1,0:T(2,128)} %precision_hbm.1, f32[2,1024]{1,0:T(2,128)} %offset_hbm.1, bf16[16,32,1024]{2,1,0:T(8,128)(2,1)} %back_ref.1), custom_call_target="tpu_custom_call" | custom-call | tf_op jit(solution)/shard_map/pallas_call | solution.py:388
  58.1 2.3 %copy.8 = bf16[16,32,1024]{2,1,0:T(8,128)(2,1)} copy(bf16[16,32,1024]{2,1,0:T(8,128)(2,1)} %shard_map.64) | data formatting | bytes 2097152

commit v4 on v3

--- a/solution.py
+++ b/solution.py
@@ -140,8 +140,8 @@
     rows,
     gram,
     leaving,
-    from_east,
-    from_west,
+    landing,
+    mine,
     stage,
     bufs,
     in_send,
@@ -152,6 +152,9 @@
     side_send,
     side_recv,
     load_sem,
+    sum_send,
+    sum_recv,
+    sum_own,
 ):
     per, values = back_ref.shape[1], back_ref.shape[2]
     count = ranks * per
@@ -179,6 +182,26 @@
     for load in loads:
         load.start()
 
+    half = ranks // 2
+    inner = jnp.logical_and(r > 0, r < ranks - 1)
+
+    def column(where, c):
+        if c == 0:
+            return half + where
+        return jnp.where(where < half, where, ranks + where)
+
+    def seat(col):
+        middle = jnp.logical_and(col >= half, col < half + ranks)
+        outer = jnp.where(col < half, col, col - ranks)
+        return jnp.where(middle, col - half, outer), jnp.where(middle, 0, 1)
+
+    side = (r // half) * half
+
+    def partner(i):
+        if i < half:
+            return half - side + lax.rem(r + i, half)
+        return side + lax.rem(r + i - half, half)
+
     barrier = pltpu.get_barrier_semaphore()
 
     def greet(where):
@@ -193,9 +216,9 @@
     pl.semaphore_wait(barrier, ranks + 1)
 
     def inward(c, i):
-        to = lax.rem(r + i, ranks)
+        to = partner(i)
         return pltpu.make_async_remote_copy(
-            src_ref=back_ref.at[2 * to + c],
+            src_ref=back_ref.at[column(to, c)],
             dst_ref=got.at[c, r],
             send_sem=in_send.at[c, i],
             recv_sem=in_recv.at[c, i],
@@ -204,10 +227,10 @@
         )
 
     def outward(c, i):
-        to = lax.rem(r + i, ranks)
+        to = partner(i)
         return pltpu.make_async_remote_copy(
             src_ref=stage.at[c, to],
-            dst_ref=out_ref.at[2 * r + c],
+            dst_ref=out_ref.at[column(r, c)],
             send_sem=out_send.at[c, i],
             recv_sem=out_recv.at[c, i],
             device_id=(g, to),
@@ -215,28 +238,64 @@
         )
 
     def own_in(c):
-        return pltpu.make_async_copy(back_ref.at[2 * r + c], got.at[c, r], own_sem.at[c])
+        return pltpu.make_async_copy(back_ref.at[column(r, c)], got.at[c, r], own_sem.at[c])
 
     def own_out(c):
-        return pltpu.make_async_copy(stage.at[c, r], out_ref.at[2 * r + c], own_sem.at[2 + c])
-
-    def sideways(k, landing, where):
+        return pltpu.make_async_copy(stage.at[c, r], out_ref.at[column(r, c)], own_sem.at[2 + c])
+
+    def sideways(c, way):
+        edge, back = (0, -1) if way == 0 else (ranks - 1, 1)
+        turn = half if way == 0 else half - 1
+        far = half - 1 if way == 0 else half
+        if c == 0:
+            group = g
+            to = jnp.where(r == edge, far, r + back)
+            phase = jnp.where(r == edge, 1, 0)
+        else:
+            group = jnp.where(r == edge, lax.rem(g + back + groups, groups), g)
+            to = jnp.where(
+                r == edge,
+                ranks - 1 - edge,
+                jnp.where(r == turn, ranks - 1 if way == 0 else 0, r + back),
+            )
+            phase = jnp.where(r == turn, 0, 1)
         return pltpu.make_async_remote_copy(
-            src_ref=leaving.at[k],
-            dst_ref=landing,
-            send_sem=side_send.at[k],
-            recv_sem=side_recv.at[k],
-            device_id=where,
+            src_ref=leaving.at[c, way],
+            dst_ref=landing.at[way, phase],
+            send_sem=side_send.at[c, way],
+            recv_sem=side_recv.at[way, phase],
+            device_id=(group, to),
             device_id_type=pl.DeviceIdType.MESH,
         )
 
-    order = list(range(1, ranks))
-    early = (len(order) + 1) // 2
+    def arrival(c, way):
+        return pltpu.make_async_remote_copy(
+            src_ref=leaving.at[c, way],
+            dst_ref=landing.at[way, c],
+            send_sem=side_send.at[c, way],
+            recv_sem=side_recv.at[way, c],
+            device_id=(g, lax.rem(r + 1, ranks)),
+            device_id_type=pl.DeviceIdType.MESH,
+        )
+
+    def sum_out(c, to, phase):
+        return pltpu.make_async_remote_copy(
+            src_ref=mine.at[c],
+            dst_ref=sums.at[phase],
+            send_sem=sum_send.at[c],
+            recv_sem=sum_recv.at[phase],
+            device_id=(g, to),
+            device_id_type=pl.DeviceIdType.MESH,
+        )
+
+    def sum_stay(c, phase):
+        return pltpu.make_async_copy(mine.at[c], sums.at[phase], sum_own.at[c])
+
+    order = [i for i in range(ranks) if i != half]
+    early, first = half//2, half//2
     for i in order:
         inward(0, i).start()
     own_in(0).start()
-    for i in order[:early]:
-        inward(1, i).start()
     own_in(1).start()
     for load in loads:
         load.wait()
@@ -263,16 +322,39 @@
             start = pl.multiple_of(t * TILE, TILE)
             value = lax.broadcasted_iota(jnp.int32, (TILE, slots.shape[1]), 0) + start
             picks = jnp.where(value == slots, 1.0, 0.0).astype(BF16)
-            sums[c, :, pl.ds(start, TILE)] = dot(high, picks, NT) + dot(low, picks, NT)
+            mine[c, :, pl.ds(start, TILE)] = dot(high, picks, NT) + dot(low, picks, NT)
             return carry
 
         lax.fori_loop(0, values // TILE, collect, 0)
+        to, phase = seat(2 * r + c)
+
+        @pl.when(to != r)
+        def _():
+            sum_out(c, to, phase).start()
+
+        @pl.when(to == r)
+        def _():
+            sum_stay(c, phase).start()
+
+    for i in order[:early]:
+        inward(1, i).start()
 
     row16 = lax.broadcasted_iota(jnp.int32, (PAD, TILE), 0)
 
     def grams(c):
+        owner = column(r, c) // 2
+        mate = lax.rem(column(r, c), 2)
+
+        @pl.when(owner != r)
+        def _():
+            sum_out(0, lax.rem(r + 1, ranks), c).wait_recv()
+
+        @pl.when(owner == r)
+        def _():
+            pltpu.make_async_copy(mine.at[mate], sums.at[c], sum_own.at[mate]).wait()
+
         own_in(c).wait()
-        for i in range(1, ranks):
+        for i in order:
             inward(c, i).wait_recv()
 
         def prepare(t, carry):
@@ -295,21 +377,14 @@
             return carry
 
         lax.fori_loop(0, values // TILE, prepare, 0)
-        for k in range(3):
-            gram[c, k * height : (k + 1) * height, :] = dot(
-                rows[k * height : (k + 1) * height, :], spread[c], NT
-            )
-
-    grams(0)
-    leaving[0] = gram[0, 0:height, :].astype(BF16)
-    westward = sideways(0, from_east, west_id)
-    westward.start()
-    for i in order[early:]:
-        inward(1, i).start()
-    grams(1)
-    leaving[1] = gram[1, 2 * height : 3 * height, :].astype(BF16)
-    eastward = sideways(1, from_west, east_id)
-    eastward.start()
+
+        def gram_of(k):
+            return dot(rows[k * height : (k + 1) * height, :], spread[c], NT)
+
+        for way, k in ((0, 0), (1, 2)):
+            leaving[c, way] = gram_of(k).astype(BF16)
+            sideways(c, way).start()
+        gram[c] = gram_of(1)
 
     square = (
         lax.broadcasted_iota(jnp.int32, (count, count), 0)
@@ -319,10 +394,14 @@
     def middle_of(x):
         return jnp.where(square, 1.5, 0.0) - 0.5 * x
 
-    def analyse(c, west_part, east_part):
+    def analyse(c):
+        for way in range(2):
+            arrival(c, way).wait_recv()
+
         def combined(start, size):
             at = pl.ds(start, size)
-            return gram[c, pl.ds(height + start, size), :] + west_part(at) + east_part(at)
+            sides = landing[0, c, at, :].astype(F32) + landing[1, c, at, :].astype(F32)
+            return gram[c, at, :] + sides
 
         system = combined(0, count) + jnp.where(square, count - 1.0, 0.0)
         pulls = combined(count, PAD)
@@ -359,22 +438,49 @@
             return carry
 
         lax.fori_loop(0, values // TILE, apply, 0)
-        for i in range(1, ranks):
+        own_out(c).start()
+
+    def release(c, which):
+        for i in which:
             outward(c, i).start()
-        own_out(c).start()
-
-    westward.wait_recv()
-    analyse(1, lambda at: gram[0, pl.ds(2 * height + at.start, at.size), :], lambda at: from_east[at, :].astype(F32))
-    eastward.wait_recv()
-    analyse(0, lambda at: from_west[at, :].astype(F32), lambda at: gram[1, at, :])
-    westward.wait_send()
-    eastward.wait_send()
+
+    grams(0)
+    for i in order[early:]:
+        inward(1, i).start()
+
+    @pl.when(inner)
+    def _():
+        analyse(0)
+        release(0, order[:first])
+
+    grams(1)
+
+    @pl.when(inner)
+    def _():
+        release(0, order[first:])
+
+    @pl.when(jnp.logical_not(inner))
+    def _():
+        analyse(0)
+        release(0, order)
+
+    analyse(1)
+    release(1, order)
+    for c in range(2):
+        to, phase = seat(2 * r + c)
+
+        @pl.when(to != r)
+        def _():
+            sum_out(c, to, phase).wait_send()
+
+        for way in range(2):
+            sideways(c, way).wait_send()
     for c in range(2):
         own_out(c).wait()
-        for i in range(1, ranks):
+        for i in order:
             inward(c, i).wait_send()
     for c in range(2):
-        for i in range(1, ranks):
+        for i in order:
             outward(c, i).wait()
 
 
@@ -401,10 +507,10 @@
             pltpu.VMEM((2, 1, values), F32),
             pltpu.VMEM((2, 8, values), F32),
             pltpu.VMEM((3 * height, values), BF16),
-            pltpu.VMEM((2, 3 * height, count), F32),
-            pltpu.VMEM((2, height, count), BF16),
-            pltpu.VMEM((height, count), BF16),
-            pltpu.VMEM((height, count), BF16),
+            pltpu.VMEM((2, height, count), F32),
+            pltpu.VMEM((2, 2, height, count), BF16),
+            pltpu.VMEM((2, 2, height, count), BF16),
+            pltpu.VMEM((2, 8, values), F32),
             pltpu.VMEM((2, ranks, per, values), BF16),
             pltpu.VMEM((2, count, count), F32),
             dma((2, ranks)),
@@ -412,9 +518,12 @@
             dma((2, ranks)),
             dma((2, ranks)),
             dma((4,)),
+            dma((2, 2)),
+            dma((2, 2)),
+            dma((5,)),
             dma((2,)),
             dma((2,)),
-            dma((5,)),
+            dma((2,)),
         ],
         compiler_params=pltpu.CompilerParams(
             collective_id=0, has_side_effects=True, vmem_limit_bytes=67043328
@@ -425,7 +534,7 @@
 def per_device(groups, ranks, background, tally, slots, datum, precision, offset):
     columns, per, values = background.shape
     whole_tiles = per % 16 == 0 and values % TILE == 0 and (ranks * per) % 128 == 0
-    if columns == 2 * ranks and whole_tiles and groups * ranks > 2:
+    if columns == 2 * ranks and whole_tiles and ranks % 2 == 0 and ranks > 2:
         return fused(groups, ranks, background, tally, slots, datum, precision, offset)
     return plain(background, tally, slots, datum, precision, offset)
 

time: 60.5 us -> 59.4 us (0.982)
  the two profiles are of different devices: /device:TPU:25 before, /device:TPU:0 now
where the time goes in v4:
time: 59.4 us; the launch traced here: 59 us
  Pallas kernels  56.7 us (95%)
  local copies, waits for them, and re-layouts  2.29 us (4%)
    pallas_call x1, Pallas kernels, fused(): pl.pallas_call(functools.partial(fused_kernel, groups, ranks), out_shape=...  56.7 us
    unnamed x1, local copies, waits for them, and re-layouts  2.29 us

profile of v4, /device:TPU:0, one launch (start us, length us, event | category | flops | bytes accessed | tf_op | source)
XLA Modules:
  0.0 59.0 jit_solution(16276933219187203237)
XLA Ops:
  0.0 56.7 %shard_map.64 = bf16[16,32,1024]{2,1,0:T(8,128)(2,1)} custom-call(s32[2]{0:T(128)} %tally_hbm.1, s32[2,1024]{1,0:T(2,128)} %slot_hbm.1, f32[2,1024]{1,0:T(2,128)} %datum_hbm.1, f32[2,1024]{1,0:T(2,128)} %precision_hbm.1, f32[2,1024]{1,0:T(2,128)} %offset_hbm.1, bf16[16,32,1024]{2,1,0:T(8,128)(2,1)} %back_ref.1), custom_call_target="tpu_custom_call" | custom-call | tf_op jit(solution)/shard_map/pallas_call | solution.py:494
  56.7 2.3 %copy.8 = bf16[16,32,1024]{2,1,0:T(8,128)(2,1)} copy(bf16[16,32,1024]{2,1,0:T(8,128)(2,1)} %shard_map.64) | data formatting | bytes 2097152
